TPU v7x, 512 devices: a whole 4x4x16 slice. The times are simulated.
512 devices in a mesh: dp: 16 (over z), expert: 32 (over x, y, core).
Axes of the slice: x: 4, y: 4, z: 16, core: 2. Of those that a mesh axis runs over, the one named last changes fastest.
Arguments:
- first_out: bfloat16 [65536, 1024], P(('dp', 'expert')), may hold values from -6 to 6
- second_out: bfloat16 [65536, 1024], P(('dp', 'expert')), may hold values from -6 to 6
- first_grad: bfloat16 [65536, 1024], P(('dp', 'expert')), may hold values from -6 to 6
- second_grad: bfloat16 [65536, 1024], P(('dp', 'expert')), may hold values from -6 to 6
- routes: int32 [65536, 2], P(('dp', 'expert')), may hold values from 0 to 31, all different within a row; in each aligned block of 128 rows (0 to 127, 128 to 255, ...) at most 16 rows name the same one
- gate_values: float32 [65536, 2], P(('dp', 'expert')), may hold values from 0.1 to 1
- w_gate: bfloat16 [32, 1024, 768], P('expert', 'dp'), may hold values from -0.1875 to 0.1875
- w_up: bfloat16 [32, 1024, 768], P('expert', 'dp'), may hold values from -0.1875 to 0.1875
- w_down: bfloat16 [32, 1024, 768], P('expert', 'dp'), may hold values from -0.21875 to 0.21875
Outputs:
- second_in: bfloat16 [65536, 1024], P(('dp', 'expert'))
- first_total: bfloat16 [65536, 1024], P(('dp', 'expert'))
- gate_grad: float32 [65536, 2], P(('dp', 'expert'))
- w_down_grad: float32 [32, 1024, 768], P('expert', 'dp')
Inputs may be any that keep to these rules, and one draw needn't show every extreme that they name: `routes`: each row names 2 different experts. Among the 128 rows of one device no expert is named more than 16 times, and in every draw some device names some expert exactly 16 times.
All inputs are finite; a program needn't handle non-finite values.
Results may differ from a plain program's by a relative error of at most 0.0051.
Values may be sent and summed in bfloat16 or wider, within the bound.
No kernel may reach another device: no remote copies, remote signals or barrier semaphores. Data moves between devices by JAX's collectives and lax.ppermute only.
A program may use at most 64 MiB of HBM per device.

v0:
```python
import math
import jax
import jax.numpy as jnp
from jax import lax
from jax.sharding import PartitionSpec as P


def expert_rows(rows_in, rows_cot, gate_mat, up_mat, down_mat):
    pre_gate = jnp.dot(rows_in, gate_mat, preferred_element_type=jnp.float32)
    pre_up = jnp.dot(rows_in, up_mat, preferred_element_type=jnp.float32)
    squashed = jax.nn.sigmoid(pre_gate)
    activated = pre_gate * squashed
    hidden = (activated * pre_up).astype(jnp.bfloat16)
    out_rows = lax.dot_general(
        hidden, down_mat, (((1,), (1,)), ((), ())), preferred_element_type=jnp.float32
    ).astype(jnp.bfloat16)
    hidden_cot = jnp.dot(rows_cot, down_mat, preferred_element_type=jnp.float32)
    gate_cot = (hidden_cot * pre_up * squashed * (1.0 + pre_gate * (1.0 - squashed))).astype(
        jnp.bfloat16
    )
    up_cot = (hidden_cot * activated).astype(jnp.bfloat16)
    input_cot = lax.dot_general(
        gate_cot, gate_mat, (((1,), (1,)), ((), ())), preferred_element_type=jnp.float32
    )
    input_cot = input_cot + lax.dot_general(
        up_cot, up_mat, (((1,), (1,)), ((), ())), preferred_element_type=jnp.float32
    )
    return (out_rows, input_cot.astype(jnp.bfloat16), hidden)


def to_slots(placing, assigned_rows):
    return lax.dot_general(
        placing, assigned_rows, (((0,), (0,)), ((), ())), preferred_element_type=jnp.float32
    ).astype(jnp.bfloat16)


def per_device(
    first_out, second_out, first_grad, second_grad, routes, gate_values, w_gate, w_up, w_down
):
    count_here = first_out.shape[0]
    feature_count = first_out.shape[1]
    top_count = routes.shape[1]
    owners = lax.axis_size("expert")
    groups = lax.axis_size("dp")
    capacity = min(count_here, 2 * count_here * top_count // owners)
    assigned = count_here * top_count
    slots_all = owners * capacity
    expert_ids = routes.reshape(assigned)
    onehot = (expert_ids[:, None] == jnp.arange(owners, dtype=jnp.int32)[None, :]).astype(jnp.int32)
    before = jnp.cumsum(onehot, axis=0) - onehot
    rank_in = jnp.sum(before * onehot, axis=1)
    slot_index = expert_ids * capacity + rank_in
    placing = (slot_index[:, None] == jnp.arange(slots_all, dtype=jnp.int32)[None, :]).astype(
        jnp.bfloat16
    )
    repeated = jnp.broadcast_to(
        first_out[:, None, :], (count_here, top_count, feature_count)
    ).reshape(assigned, feature_count)
    grad_repeated = jnp.broadcast_to(
        second_grad[:, None, :], (count_here, top_count, feature_count)
    ).reshape(assigned, feature_count)
    cot_rows = (gate_values.reshape(assigned)[:, None] * grad_repeated.astype(jnp.float32)).astype(
        jnp.bfloat16
    )
    send_input = to_slots(placing, repeated).reshape(owners, capacity, feature_count)
    send_cot = to_slots(placing, cot_rows).reshape(owners, capacity, feature_count)
    arrived_input, arrived_cot = (
        lax.all_to_all(send_input, "expert", split_axis=0, concat_axis=0, tiled=True),
        lax.all_to_all(send_cot, "expert", split_axis=0, concat_axis=0, tiled=True),
    )
    rows_in = arrived_input.reshape(slots_all, feature_count)
    rows_cot = arrived_cot.reshape(slots_all, feature_count)
    hidden_count = w_gate.shape[2]
    shards = jnp.concatenate([w_gate[0], w_up[0], w_down[0]], axis=1)
    mats = lax.all_gather(shards, "dp", axis=0, tiled=True)
    gate_mat = mats[:, :hidden_count]
    up_mat = mats[:, hidden_count : 2 * hidden_count]
    down_mat = mats[:, 2 * hidden_count :]
    out_rows, input_cot, hidden = expert_rows(rows_in, rows_cot, gate_mat, up_mat, down_mat)
    grad_scale = 1.0 / math.sqrt(count_here * groups)
    partial_grad = lax.dot_general(
        rows_cot, hidden, (((0,), (0,)), ((), ())), preferred_element_type=jnp.float32
    )
    reduced = lax.psum_scatter(partial_grad, "dp", scatter_dimension=0, tiled=True)
    w_down_grad = (reduced * grad_scale)[None]
    back_out, back_cot = (
        lax.all_to_all(
            out_rows.reshape(owners, capacity, feature_count),
            "expert",
            split_axis=0,
            concat_axis=0,
            tiled=True,
        ),
        lax.all_to_all(
            input_cot.reshape(owners, capacity, feature_count),
            "expert",
            split_axis=0,
            concat_axis=0,
            tiled=True,
        ),
    )
    out_assigned = jnp.dot(
        placing, back_out.reshape(slots_all, feature_count), preferred_element_type=jnp.float32
    )
    cot_assigned = jnp.dot(
        placing, back_cot.reshape(slots_all, feature_count), preferred_element_type=jnp.float32
    )
    expert_out = out_assigned.reshape(count_here, top_count, feature_count)
    combined = jnp.sum(gate_values[:, :, None] * expert_out, axis=1)
    second_in = (second_out.astype(jnp.float32) - combined).astype(jnp.bfloat16)
    gate_grad = jnp.sum(second_grad.astype(jnp.float32)[:, None, :] * expert_out, axis=2)
    first_total = (
        first_grad.astype(jnp.float32)
        + jnp.sum(cot_assigned.reshape(count_here, top_count, feature_count), axis=1)
    ).astype(jnp.bfloat16)
    return (second_in, first_total, gate_grad, w_down_grad)


def solution(mesh):
    placed = (
        P(("dp", "expert"), None),
        P(("dp", "expert"), None),
        P(("dp", "expert"), None),
        P(("dp", "expert"), None),
        P(("dp", "expert"), None),
        P(("dp", "expert"), None),
        P("expert", "dp", None),
        P("expert", "dp", None),
        P("expert", "dp", None),
    )
    return jax.shard_map(
        per_device,
        mesh=mesh,
        in_specs=placed,
        out_specs=(
            P(("dp", "expert"), None),
            P(("dp", "expert"), None),
            P(("dp", "expert"), None),
            P("expert", "dp", None),
        ),
        check_vma=False,
    )
```

profile of v0, /device:TPU:2, one launch (start us, length us, event | category | flops | bytes accessed | tf_op | source)
XLA Modules:
  0.0 185.1 jit_solution(12592394571378709768)
XLA Ops:
  7.2 1.7 pad_maximum_fusion
  9.0 0.8 copy.21
  10.9 1.2 broadcast_in_dim.6
  12.4 1.5 convolution_convert_fusion.2
  14.0 9.5 %all-to-all-start = ((bf16[32,16,1024]{2,1,0:T(8,128)(2,1)}), bf16[32,16,1024]{2,1,0:T(8,128)(2,1)S(1)}, u32[]{:S(2)}, u32[]{:S(2)}) async-start(bf16[32,16,1024]{2,1,0:T(8,128)(2,1)} %bitcast.2), calls=%async_computation | async-start | bytes 2097152 | tf_op jit(solution)/shard_map/all_to_all | solution.py:68
  24.8 1.6 convolution_convert_fusion.1
  26.4 11.6 %all-to-all-done = bf16[32,16,1024]{2,1,0:T(8,128)(2,1)S(1)} async-done(((bf16[32,16,1024]{2,1,0:T(8,128)(2,1)}), bf16[32,16,1024]{2,1,0:T(8,128)(2,1)S(1)}, u32[]{:S(2)}, u32[]{:S(2)}) %all-to-all-start) | async-done | bytes 1048608 | tf_op jit(solution)/shard_map/all_to_all | solution.py:68
  38.0 6.4 %all-to-all-start.2 = ((bf16[32,16,1024]{2,1,0:T(8,128)(2,1)}), bf16[32,16,1024]{2,1,0:T(8,128)(2,1)S(1)}, u32[]{:S(2)}, u32[]{:S(2)}) async-start(bf16[32,16,1024]{2,1,0:T(8,128)(2,1)} %bitcast.10), calls=%async_computation.2 | async-start | bytes 2097152 | tf_op jit(solution)/shard_map/all_to_all | solution.py:69
  44.4 49.0 %all-gather.2.cloned.1.call-done = bf16[1024,2304]{1,0:T(8,128)(2,1)} async-done(((bf16[64,2304]{1,0:T(8,128)(2,1)}), bf16[1024,2304]{1,0:T(8,128)(2,1)}) %all-gather.2.cloned.1.call-update) | async-done | bytes 4718608 | tf_op jit(solution)/shard_map/all_gather | solution.py:75
  93.5 2.4 %fusion.9 = f32[512,768]{1,0:T(8,128)S(1)} fusion(bf16[512,1024]{1,0:T(8,128)(2,1)S(1)} %bitcast.53, bf16[1024,2304]{1,0:T(8,128)(2,1)} %all-gather.2.cloned.1.call-done), kind=kOutput, calls=%fused_computation.17 | convolution fusion | flops 805306368 | bytes 4194304 | tf_op jit(solution)/shard_map/dot_general | solution.py:9
  95.9 1.2 copy-done.5
  97.0 3.6 %multiply_convert_fusion.2 = (bf16[512,768]{1,0:T(8,128)(2,1)S(1)}, f32[512,768]{1,0:T(8,128)}) fusion(f32[512,768]{1,0:T(8,128)S(1)} %fusion.9, bf16[512,1024]{1,0:T(8,128)(2,1)S(1)} %bitcast.54, bf16[1024,2304]{1,0:T(8,128)(2,1)} %all-gather.2.cloned.1.call-done), kind=kOutput, calls=%fused_computation.3 | convolution fusion | flops 807665664 | bytes 6553600 | tf_op jit(solution)/shard_map/dot_general | solution.py:10
  100.7 2.7 %fusion.27 = f32[1024,768]{1,0:T(8,128)} fusion(bf16[512,1024]{1,0:T(8,128)(2,1)S(1)} %bitcast.51, bf16[512,768]{1,0:T(8,128)(2,1)S(1)} %get-tuple-element.6), kind=kOutput, calls=%fused_computation.49 | convolution fusion | flops 805306368 | bytes 4980736 | tf_op jit(solution)/shard_map/dot_general | solution.py:81
  103.4 2.5 %fusion.1 = f32[512,768]{1,0:T(8,128)S(1)} fusion(bf16[512,1024]{1,0:T(8,128)(2,1)S(1)} %bitcast.52, bf16[1024,2304]{1,0:T(8,128)(2,1)} %all-gather.2.cloned.1.call-done), kind=kOutput, calls=%fused_computation.9 | convolution fusion | flops 805306368 | bytes 4194304 | tf_op jit(solution)/shard_map/dot_general | solution.py:17
  106.0 2.9 %fusion.7 = f32[512,1024]{1,0:T(8,128)S(1)} fusion(bf16[1024,2304]{1,0:T(8,128)(2,1)} %all-gather.2.cloned.1.call-done, f32[512,768]{1,0:T(8,128)S(1)} %copy-done.6, f32[512,768]{1,0:T(8,128)S(1)} %fusion.1, f32[512,768]{1,0:T(8,128)S(1)} %copy-done.7), kind=kOutput, calls=%fused_computation.15 | convolution fusion | flops 809238528 | bytes 8388608 | tf_op jit(solution)/shard_map/dot_general | solution.py:22
  108.8 3.5 %add_convert_fusion = bf16[512,1024]{1,0:T(8,128)(2,1)} fusion(f32[512,1024]{1,0:T(8,128)S(1)} %fusion.7, bf16[1024,2304]{1,0:T(8,128)(2,1)} %all-gather.2.cloned.1.call-done, f32[512,768]{1,0:T(8,128)S(1)} %fusion.1, f32[512,768]{1,0:T(8,128)S(1)} %copy-done.6), kind=kOutput, calls=%fused_computation | convolution fusion | flops 808714240 | bytes 7864320 | tf_op jit(solution)/shard_map/dot_general | solution.py:25
  112.3 7.7 %all-to-all-start.3 = ((bf16[32,16,1024]{2,1,0:T(8,128)(2,1)}), bf16[32,16,1024]{2,1,0:T(8,128)(2,1)S(1)}, u32[]{:S(2)}, u32[]{:S(2)}) async-start(bf16[32,16,1024]{2,1,0:T(8,128)(2,1)} %bitcast.12), calls=%async_computation.3 | async-start | bytes 2097152 | tf_op jit(solution)/shard_map/all_to_all | solution.py:94
  120.1 3.5 %convolution_convert_fusion = bf16[512,1024]{1,0:T(8,128)(2,1)} fusion(bf16[512,768]{1,0:T(8,128)(2,1)S(1)} %get-tuple-element.6, bf16[1024,2304]{1,0:T(8,128)(2,1)} %all-gather.2.cloned.1.call-done), kind=kOutput, calls=%fused_computation.6 | convolution fusion | flops 805830656 | bytes 3407872 | tf_op jit(solution)/shard_map/dot_general | solution.py:14
  123.5 10.9 %all-to-all-done.3 = bf16[32,16,1024]{2,1,0:T(8,128)(2,1)S(1)} async-done(((bf16[32,16,1024]{2,1,0:T(8,128)(2,1)}), bf16[32,16,1024]{2,1,0:T(8,128)(2,1)S(1)}, u32[]{:S(2)}, u32[]{:S(2)}) %all-to-all-start.3) | async-done | bytes 1048608 | tf_op jit(solution)/shard_map/all_to_all | solution.py:94
  134.5 6.4 %all-to-all-start.1 = ((bf16[32,16,1024]{2,1,0:T(8,128)(2,1)}), bf16[32,16,1024]{2,1,0:T(8,128)(2,1)S(1)}, u32[]{:S(2)}, u32[]{:S(2)}) async-start(bf16[32,16,1024]{2,1,0:T(8,128)(2,1)} %bitcast.7), calls=%async_computation.1 | async-start | bytes 2097152 | tf_op jit(solution)/shard_map/all_to_all | solution.py:87
  141.7 13.6 %all-to-all-done.1 = bf16[32,16,1024]{2,1,0:T(8,128)(2,1)S(1)} async-done(((bf16[32,16,1024]{2,1,0:T(8,128)(2,1)}), bf16[32,16,1024]{2,1,0:T(8,128)(2,1)S(1)}, u32[]{:S(2)}, u32[]{:S(2)}) %all-to-all-start.1) | async-done | bytes 1048608 | tf_op jit(solution)/shard_map/all_to_all | solution.py:87
  155.3 1.1 multiply_reduce_fusion
  158.0 18.7 %reduce-scatter.2.cloned.1.call-done = f32[64,768]{1,0:T(8,128)} async-done(((f32[1024,768]{1,0:T(8,128)}), f32[64,768]{1,0:T(8,128)}) %reduce-scatter.2.cloned.1.call-update) | async-done | bytes 196624 | tf_op jit(solution)/shard_map/reduce_scatter | solution.py:84
  176.7 1.6 multiply_bitcast_fusion
  (41 shorter events, 5.1 us)
Async XLA Ops:
  7.2 86.3 %all-gather.2.cloned.1.call-start = ((), (), s32[]{:S(2)}) async-start(), calls=%async_computation.5 | async-start | bytes 5013504 | tf_op jit(solution)/shard_map/all_gather | solution.py:75
  12.4 11.1 %copy-start = (bf16[128,1024]{1,0:T(8,128)(2,1)S(1)}, bf16[128,1024]{1,0:T(8,128)(2,1)}, u32[]{:S(2)}) copy-start(bf16[128,1024]{1,0:T(8,128)(2,1)} %param.12) | copy-start | bytes 786436
  14.0 24.0 %all-to-all-start = ((bf16[32,16,1024]{2,1,0:T(8,128)(2,1)}), bf16[32,16,1024]{2,1,0:T(8,128)(2,1)S(1)}, u32[]{:S(2)}, u32[]{:S(2)}) async-start(bf16[32,16,1024]{2,1,0:T(8,128)(2,1)} %bitcast.2), calls=%async_computation | async-start | bytes 2097152 | tf_op jit(solution)/shard_map/all_to_all | solution.py:68
  23.5 1.0 copy-start.4
  38.0 62.7 %all-to-all-start.2 = ((bf16[32,16,1024]{2,1,0:T(8,128)(2,1)}), bf16[32,16,1024]{2,1,0:T(8,128)(2,1)S(1)}, u32[]{:S(2)}, u32[]{:S(2)}) async-start(bf16[32,16,1024]{2,1,0:T(8,128)(2,1)} %bitcast.10), calls=%async_computation.2 | async-start | bytes 2097152 | tf_op jit(solution)/shard_map/all_to_all | solution.py:69
  44.4 132.3 %reduce-scatter.2.cloned.1.call-start = ((), (), s32[]{:S(2)}) async-start(), calls=%async_computation.6 | async-start | bytes 3342336 | tf_op jit(solution)/shard_map/reduce_scatter | solution.py:84
  95.8 1.2 copy-start.5
  103.4 2.6 %copy-start.6 = (f32[512,768]{1,0:T(8,128)S(1)}, f32[512,768]{1,0:T(8,128)}, u32[]{:S(2)}) copy-start(f32[512,768]{1,0:T(8,128)} %copy-done.5) | copy-start | bytes 4718596
  103.4 2.6 %copy-start.7 = (f32[512,768]{1,0:T(8,128)S(1)}, f32[512,768]{1,0:T(8,128)}, u32[]{:S(2)}) copy-start(f32[512,768]{1,0:T(8,128)} %get-tuple-element.7) | copy-start | bytes 4718596
  112.3 22.1 %all-to-all-start.3 = ((bf16[32,16,1024]{2,1,0:T(8,128)(2,1)}), bf16[32,16,1024]{2,1,0:T(8,128)(2,1)S(1)}, u32[]{:S(2)}, u32[]{:S(2)}) async-start(bf16[32,16,1024]{2,1,0:T(8,128)(2,1)} %bitcast.12), calls=%async_computation.3 | async-start | bytes 2097152 | tf_op jit(solution)/shard_map/all_to_all | solution.py:94
  123.5 17.6 %copy-start.3 = (s32[128,2]{0,1:T(2,128)S(1)}, s32[128,2]{0,1:T(2,128)}, u32[]{:S(2)}) copy-start(s32[128,2]{0,1:T(2,128)} %param.13) | copy-start | bytes 3076
  134.5 20.8 %all-to-all-start.1 = ((bf16[32,16,1024]{2,1,0:T(8,128)(2,1)}), bf16[32,16,1024]{2,1,0:T(8,128)(2,1)S(1)}, u32[]{:S(2)}, u32[]{:S(2)}) async-start(bf16[32,16,1024]{2,1,0:T(8,128)(2,1)} %bitcast.7), calls=%async_computation.1 | async-start | bytes 2097152 | tf_op jit(solution)/shard_map/all_to_all | solution.py:87
  141.7 14.8 %copy-start.1 = (bf16[128,1024]{1,0:T(8,128)(2,1)S(1)}, bf16[128,1024]{1,0:T(8,128)(2,1)}, u32[]{:S(2)}) copy-start(bf16[128,1024]{1,0:T(8,128)(2,1)} %param.11) | copy-start | bytes 786436
  155.3 1.9 %copy-start.2 = (bf16[128,1024]{1,0:T(8,128)(2,1)S(1)}, bf16[128,1024]{1,0:T(8,128)(2,1)}, u32[]{:S(2)}) copy-start(bf16[128,1024]{1,0:T(8,128)(2,1)} %param.10) | copy-start | bytes 786436
Sparse Core Ops, SparseCore 0:
  10.1 83.3 all-gather.1
  103.5 73.1 reduce-scatter.1
where the time goes:
time: 186 us; the launch traced here: 185 us
  waiting for transfers between devices  104 us (56%)
  starting transfers between devices  30.1 us (16%)
  matrix products  25.9 us (14%)
  between operations  14.3 us (8%)
  other arithmetic  5.66 us (3%)
  local copies, waits for them, and re-layouts  5.32 us (3%)
    all_gather x1, waiting for transfers between devices, per_device(): mats = lax.all_gather(shards, 'dp', axis=0, tiled=True)  49 us
    reduce_scatter x1, waiting for transfers between devices, per_device(): lax.psum_scatter(partial_grad, 'dp', scatter_dimension=0, tiled=True)  18.7 us
    all_to_all x1, waiting for transfers between devices, per_device(): lax.all_to_all(out_rows.reshape(owners, capacity, feature_count), 'expert...  13.6 us
    all_to_all x1, waiting for transfers between devices, per_device(): lax.all_to_all(send_input, 'expert', split_axis=0, concat_axis=0, tiled=T...  11.6 us
    all_to_all x1, waiting for transfers between devices, per_device(): lax.all_to_all(input_cot.reshape(owners, capacity, feature_count), 'exper...  10.9 us
    all_to_all x1, starting transfers between devices, per_device(): lax.all_to_all(send_input, 'expert', split_axis=0, concat_axis=0, tiled=T...  9.51 us
    all_to_all x1, starting transfers between devices, per_device(): lax.all_to_all(input_cot.reshape(owners, capacity, feature_count), 'exper...  7.71 us
    all_to_all x1, starting transfers between devices, per_device(): lax.all_to_all(out_rows.reshape(owners, capacity, feature_count), 'expert...  6.42 us
  transfers between devices with their start and end apart: 6, of which 5 were waited for; matrix products, arithmetic and copies ran while one was open for 16% of the time, Pallas kernels for 0%

commit v1 on v0

--- a/solution.py
+++ b/solution.py
@@ -72,7 +72,9 @@
     rows_cot = arrived_cot.reshape(slots_all, feature_count)
     hidden_count = w_gate.shape[2]
     shards = jnp.concatenate([w_gate[0], w_up[0], w_down[0]], axis=1)
-    mats = lax.all_gather(shards, "dp", axis=0, tiled=True)
+    mats = jnp.concatenate(
+        lax.all_to_all(jnp.stack([shards] * lax.axis_size("dp")), "dp", 0, 0), axis=0
+    )
     gate_mat = mats[:, :hidden_count]
     up_mat = mats[:, hidden_count : 2 * hidden_count]
     down_mat = mats[:, 2 * hidden_count :]

time: 186 us -> 366 us (1.97)
  the two profiles are of different devices: /device:TPU:2 before, /device:TPU:14 now
where the time goes in v1:
time: 366 us; the launch traced here: 365 us
  waiting for transfers between devices  269 us (73%)
  starting transfers between devices  44.1 us (12%)
  matrix products  25.9 us (7%)
  between operations  14.3 us (4%)
  local copies, waits for them, and re-layouts  7.93 us (2%)
  other arithmetic  3.95 us (1%)
    all_to_all x1, waiting for transfers between devices, per_device(): lax.all_to_all(jnp.stack([shards] * lax.axis_size('dp')), 'dp', 0, 0)  203 us
    reduce_scatter x1, waiting for transfers between devices, per_device(): lax.psum_scatter(partial_grad, 'dp', scatter_dimension=0, tiled=True)  23.3 us
    all_to_all x1, waiting for transfers between devices, per_device(): lax.all_to_all(send_input, 'expert', split_axis=0, concat_axis=0, tiled=T...  13.6 us
    all_to_all x1, starting transfers between devices, per_device(): lax.all_to_all(jnp.stack([shards] * lax.axis_size('dp')), 'dp', 0, 0)  13.5 us
    all_to_all x1, waiting for transfers between devices, per_device(): lax.all_to_all(out_rows.reshape(owners, capacity, feature_count), 'expert...  12.9 us
    all_to_all x1, waiting for transfers between devices, per_device(): lax.all_to_all(input_cot.reshape(owners, capacity, feature_count), 'exper...  10.2 us
    all_to_all x1, starting transfers between devices, per_device(): lax.all_to_all(send_input, 'expert', split_axis=0, concat_axis=0, tiled=T...  9.46 us
  transfers between devices with their start and end apart: 6, of which 6 were waited for; matrix products, arithmetic and copies ran while one was open for 7% of the time, Pallas kernels for 0%

profile of v1, /device:TPU:14, one launch (start us, length us, event | category | flops | bytes accessed | tf_op | source)
XLA Modules:
  0.0 365.2 jit_solution(5244677446537519914)
XLA Ops:
  9.2 1.2 broadcast_in_dim.6
  10.7 1.5 convolution_convert_fusion.2
  12.2 9.5 %all-to-all-start = ((bf16[32,16,1024]{2,1,0:T(8,128)(2,1)}), bf16[32,16,1024]{2,1,0:T(8,128)(2,1)S(1)}, u32[]{:S(2)}, u32[]{:S(2)}) async-start(bf16[32,16,1024]{2,1,0:T(8,128)(2,1)} %bitcast.2), calls=%async_computation | async-start | bytes 2097152 | tf_op jit(solution)/shard_map/all_to_all | solution.py:68
  21.7 13.6 %all-to-all-done = bf16[32,16,1024]{2,1,0:T(8,128)(2,1)S(1)} async-done(((bf16[32,16,1024]{2,1,0:T(8,128)(2,1)}), bf16[32,16,1024]{2,1,0:T(8,128)(2,1)S(1)}, u32[]{:S(2)}, u32[]{:S(2)}) %all-to-all-start) | async-done | bytes 1048608 | tf_op jit(solution)/shard_map/all_to_all | solution.py:68
  35.3 2.6 stack.2
  37.9 13.5 %all-to-all-start.1 = ((bf16[16,64,2304]{2,1,0:T(8,128)(2,1)}), bf16[16,64,2304]{2,1,0:T(8,128)(2,1)}, u32[]{:S(2)}, u32[]{:S(2)}) async-start(bf16[16,64,2304]{2,1,0:T(8,128)(2,1)} %stack.2), calls=%async_computation.1 | async-start | bytes 9437184 | tf_op jit(solution)/shard_map/all_to_all | solution.py:76
  52.7 1.6 convolution_convert_fusion.1
  54.3 202.6 %all-to-all-done.1 = bf16[16,64,2304]{2,1,0:T(8,128)(2,1)} async-done(((bf16[16,64,2304]{2,1,0:T(8,128)(2,1)}), bf16[16,64,2304]{2,1,0:T(8,128)(2,1)}, u32[]{:S(2)}, u32[]{:S(2)}) %all-to-all-start.1) | async-done | bytes 4718624 | tf_op jit(solution)/shard_map/all_to_all | solution.py:76
  256.9 6.9 %all-to-all-start.3 = ((bf16[32,16,1024]{2,1,0:T(8,128)(2,1)}), bf16[32,16,1024]{2,1,0:T(8,128)(2,1)S(1)}, u32[]{:S(2)}, u32[]{:S(2)}) async-start(bf16[32,16,1024]{2,1,0:T(8,128)(2,1)} %bitcast.11), calls=%async_computation.3 | async-start | bytes 2097152 | tf_op jit(solution)/shard_map/all_to_all | solution.py:69
  263.8 2.4 fusion.9
  267.4 3.7 %multiply_convert_fusion.2 = (bf16[512,768]{1,0:T(8,128)(2,1)S(1)}, f32[512,768]{1,0:T(8,128)}) fusion(f32[512,768]{1,0:T(8,128)S(1)} %fusion.9, bf16[512,1024]{1,0:T(8,128)(2,1)S(1)} %bitcast.55, bf16[1024,2304]{1,0:T(8,128)(2,1)} %bitcast.7), kind=kOutput, calls=%fused_computation.3 | convolution fusion | flops 807665664 | bytes 6553600 | tf_op jit(solution)/shard_map/dot_general | solution.py:10
  271.0 6.4 %all-to-all-done.3 = bf16[32,16,1024]{2,1,0:T(8,128)(2,1)S(1)} async-done(((bf16[32,16,1024]{2,1,0:T(8,128)(2,1)}), bf16[32,16,1024]{2,1,0:T(8,128)(2,1)S(1)}, u32[]{:S(2)}, u32[]{:S(2)}) %all-to-all-start.3) | async-done | bytes 1048608 | tf_op jit(solution)/shard_map/all_to_all | solution.py:69
  277.4 2.7 fusion.27
  280.1 2.5 fusion.1
  282.7 2.9 fusion.7
  285.6 3.4 add_convert_fusion
  289.1 7.1 %all-to-all-start.4 = ((bf16[32,16,1024]{2,1,0:T(8,128)(2,1)}), bf16[32,16,1024]{2,1,0:T(8,128)(2,1)S(1)}, u32[]{:S(2)}, u32[]{:S(2)}) async-start(bf16[32,16,1024]{2,1,0:T(8,128)(2,1)} %bitcast.13), calls=%async_computation.4 | async-start | bytes 2097152 | tf_op jit(solution)/shard_map/all_to_all | solution.py:96
  296.2 3.5 convolution_convert_fusion
  299.7 10.2 %all-to-all-done.4 = bf16[32,16,1024]{2,1,0:T(8,128)(2,1)S(1)} async-done(((bf16[32,16,1024]{2,1,0:T(8,128)(2,1)}), bf16[32,16,1024]{2,1,0:T(8,128)(2,1)S(1)}, u32[]{:S(2)}, u32[]{:S(2)}) %all-to-all-start.4) | async-done | bytes 1048608 | tf_op jit(solution)/shard_map/all_to_all | solution.py:96
  309.9 7.1 %all-to-all-start.2 = ((bf16[32,16,1024]{2,1,0:T(8,128)(2,1)}), bf16[32,16,1024]{2,1,0:T(8,128)(2,1)S(1)}, u32[]{:S(2)}, u32[]{:S(2)}) async-start(bf16[32,16,1024]{2,1,0:T(8,128)(2,1)} %bitcast.8), calls=%async_computation.2 | async-start | bytes 2097152 | tf_op jit(solution)/shard_map/all_to_all | solution.py:89
  317.8 12.9 %all-to-all-done.2 = bf16[32,16,1024]{2,1,0:T(8,128)(2,1)S(1)} async-done(((bf16[32,16,1024]{2,1,0:T(8,128)(2,1)}), bf16[32,16,1024]{2,1,0:T(8,128)(2,1)S(1)}, u32[]{:S(2)}, u32[]{:S(2)}) %all-to-all-start.2) | async-done | bytes 1048608 | tf_op jit(solution)/shard_map/all_to_all | solution.py:89
  330.7 1.1 multiply_reduce_fusion
  333.4 23.3 %reduce-scatter.2.cloned.1.call-done = f32[64,768]{1,0:T(8,128)} async-done(((f32[1024,768]{1,0:T(8,128)}), f32[64,768]{1,0:T(8,128)}) %reduce-scatter.2.cloned.1.call-update) | async-done | bytes 196624 | tf_op jit(solution)/shard_map/reduce_scatter | solution.py:86
  356.8 1.6 multiply_bitcast_fusion
  (47 shorter events, 7.0 us)
Async XLA Ops:
  10.6 11.0 %copy-start.3 = (bf16[1,64,768]{2,1,0:T(8,128)(2,1)S(1)}, bf16[1,64,768]{2,1,0:T(8,128)(2,1)}, u32[]{:S(2)}) copy-start(bf16[1,64,768]{2,1,0:T(8,128)(2,1)} %param.17) | copy-start | bytes 294916
  10.6 11.0 %copy-start.4 = (bf16[1,64,768]{2,1,0:T(8,128)(2,1)S(1)}, bf16[1,64,768]{2,1,0:T(8,128)(2,1)}, u32[]{:S(2)}) copy-start(bf16[1,64,768]{2,1,0:T(8,128)(2,1)} %param.16) | copy-start | bytes 294916
  10.6 11.0 %copy-start.5 = (bf16[1,64,768]{2,1,0:T(8,128)(2,1)S(1)}, bf16[1,64,768]{2,1,0:T(8,128)(2,1)}, u32[]{:S(2)}) copy-start(bf16[1,64,768]{2,1,0:T(8,128)(2,1)} %param.15) | copy-start | bytes 294916
  12.2 23.1 %all-to-all-start = ((bf16[32,16,1024]{2,1,0:T(8,128)(2,1)}), bf16[32,16,1024]{2,1,0:T(8,128)(2,1)S(1)}, u32[]{:S(2)}, u32[]{:S(2)}) async-start(bf16[32,16,1024]{2,1,0:T(8,128)(2,1)} %bitcast.2), calls=%async_computation | async-start | bytes 2097152 | tf_op jit(solution)/shard_map/all_to_all | solution.py:68
  37.9 13.5 %copy-start = (bf16[128,1024]{1,0:T(8,128)(2,1)S(1)}, bf16[128,1024]{1,0:T(8,128)(2,1)}, u32[]{:S(2)}) copy-start(bf16[128,1024]{1,0:T(8,128)(2,1)} %param.12) | copy-start | bytes 786436
  37.9 218.9 %all-to-all-start.1 = ((bf16[16,64,2304]{2,1,0:T(8,128)(2,1)}), bf16[16,64,2304]{2,1,0:T(8,128)(2,1)}, u32[]{:S(2)}, u32[]{:S(2)}) async-start(bf16[16,64,2304]{2,1,0:T(8,128)(2,1)} %stack.2), calls=%async_computation.1 | async-start | bytes 9437184 | tf_op jit(solution)/shard_map/all_to_all | solution.py:76
  51.4 1.0 copy-start.7
  256.9 20.5 %all-to-all-start.3 = ((bf16[32,16,1024]{2,1,0:T(8,128)(2,1)}), bf16[32,16,1024]{2,1,0:T(8,128)(2,1)S(1)}, u32[]{:S(2)}, u32[]{:S(2)}) async-start(bf16[32,16,1024]{2,1,0:T(8,128)(2,1)} %bitcast.11), calls=%async_computation.3 | async-start | bytes 2097152 | tf_op jit(solution)/shard_map/all_to_all | solution.py:69
  263.8 93.0 %reduce-scatter.2.cloned.1.call-start = ((), (), s32[]{:S(2)}) async-start(), calls=%async_computation.6 | async-start | bytes 3342336 | tf_op jit(solution)/shard_map/reduce_scatter | solution.py:86
  266.2 1.1 copy-start.8
  280.1 2.6 copy-start.9
  280.1 2.6 copy-start.10
  289.1 20.9 %all-to-all-start.4 = ((bf16[32,16,1024]{2,1,0:T(8,128)(2,1)}), bf16[32,16,1024]{2,1,0:T(8,128)(2,1)S(1)}, u32[]{:S(2)}, u32[]{:S(2)}) async-start(bf16[32,16,1024]{2,1,0:T(8,128)(2,1)} %bitcast.13), calls=%async_computation.4 | async-start | bytes 2097152 | tf_op jit(solution)/shard_map/all_to_all | solution.py:96
  299.7 17.6 %copy-start.6 = (s32[128,2]{0,1:T(2,128)S(1)}, s32[128,2]{0,1:T(2,128)}, u32[]{:S(2)}) copy-start(s32[128,2]{0,1:T(2,128)} %param.13) | copy-start | bytes 3076
  309.9 20.8 %all-to-all-start.2 = ((bf16[32,16,1024]{2,1,0:T(8,128)(2,1)}), bf16[32,16,1024]{2,1,0:T(8,128)(2,1)S(1)}, u32[]{:S(2)}, u32[]{:S(2)}) async-start(bf16[32,16,1024]{2,1,0:T(8,128)(2,1)} %bitcast.8), calls=%async_computation.2 | async-start | bytes 2097152 | tf_op jit(solution)/shard_map/all_to_all | solution.py:89
  317.8 14.1 %copy-start.1 = (bf16[128,1024]{1,0:T(8,128)(2,1)S(1)}, bf16[128,1024]{1,0:T(8,128)(2,1)}, u32[]{:S(2)}) copy-start(bf16[128,1024]{1,0:T(8,128)(2,1)} %param.11) | copy-start | bytes 786436
  330.7 1.9 copy-start.2
Sparse Core Ops, SparseCore 0:
  280.2 76.4 reduce-scatter.1
